TPU v7x, 512 devices: a whole 4x8x8 slice. The times are simulated.
512 devices in a mesh: tiles: 128 (over y, z, core), rep: 4 (over x).
Axes of the slice: x: 4, y: 8, z: 8, core: 2. Of those that a mesh axis runs over, the one named last changes fastest.
Arguments:
- dissim: float32 [17408, 128, 128], P(('tiles', 'rep')), may hold values from 0.5 to 4
- tile_map: int32 [17408, 2], P(('tiles', 'rep')), may hold values from -1 to 127, as said below
- owned_blocks: int32 [128], P('tiles'), may hold values from 0 to 127, each once
- start_coords: float32 [128, 3, 128], P('tiles'), may hold values from -6 to 6
Outputs:
- coords: float32 [128, 3, 128], P('tiles')
- stress: float32 [], replicated
Inputs may be any that keep to these rules, and one draw needn't show every extreme that they name: `tile_map`: every pair (r, c) with 0 <= r <= c < 128 stands in exactly one row; every other row is (-1, -1); the 34 rows of one device are filled by between 0 and 34 tiles, and one device is full.
All inputs are finite; a program needn't handle non-finite values.
Results may differ from a plain program's by a relative error of at most 0.0003.
Values sent between devices are 32-bit elements; how exact they have to be, the bound alone decides.
A program may use at most 64 MiB of HBM per device.

v0:
```python
import functools

import jax
import jax.numpy as jnp
from jax import lax
from jax.sharding import Mesh
from jax.sharding import PartitionSpec as P

ITERS = 3
TILES = ("tiles_0", "tiles_1", "tiles_2")
TILES_REP = ("tiles_0", "tiles_1", "tiles_2", "rep")


distance_floor = 0.25


def from_everyone(array, axis):
    copies = jnp.broadcast_to(array, (lax.axis_size(axis), *array.shape))
    return lax.all_to_all(copies, axis, split_axis=0, concat_axis=0, tiled=True)


def joined_along(parts, dim):
    parts = jnp.moveaxis(parts, 0, dim)
    dims = parts.shape
    return parts.reshape(*dims[:dim], dims[dim] * dims[dim + 1], *dims[dim + 2 :])


def whole_of(array, axes, dim):
    far, near = axes
    initial = from_everyone(array, far)
    parts = jnp.swapaxes(from_everyone(initial, near), 0, 1)
    return joined_along(parts.reshape(-1, *array.shape), dim)


def over_axes(array, axes):
    return functools.reduce(lax.psum, axes, array)


def cut_along(array, dim, peers):
    before, after = (array.shape[:dim], array.shape[dim + 1 :])
    return jnp.moveaxis(array.reshape(*before, peers, -1, *after), dim, 0)


def summed_on_arrival(array, axis, dim):
    peers = lax.axis_size(axis)
    parts = lax.all_to_all(cut_along(array, dim, peers), axis, 0, 0, tiled=True)
    return jnp.sum(parts, axis=0)


def sum_by_axis(array, axes, dim):
    far, near = axes
    own = summed_on_arrival(cut_along(array, dim, lax.axis_size(far)), near, dim + 1)
    return jnp.sum(lax.all_to_all(own, far, 0, 0, tiled=True), axis=0)


def filled_up(lines, peers):
    spare = -lines.shape[0] % peers
    if not spare:
        return lines
    return jnp.concatenate([lines, jnp.zeros((spare, *lines.shape[1:]), lines.dtype)])


def total_of(array, axes):
    lines = array.reshape(-1)
    own = sum_by_axis(filled_up(lines, lax.axis_size(axes[0]) * lax.axis_size(axes[1])), axes, 0)
    whole = whole_of(own, axes, 0)
    return whole[: len(lines)].reshape(array.shape)


def tile_terms(coords_all, dissim, tile_map, slot_of):
    row_ids = tile_map[:, 0]
    col_ids = tile_map[:, 1]
    occupied = row_ids >= 0
    row_slot = slot_of[jnp.maximum(row_ids, 0)]
    col_slot = slot_of[jnp.maximum(col_ids, 0)]
    row_points = coords_all[row_slot]
    col_points = coords_all[col_slot]
    tile_width = dissim.shape[1]
    offsets = jnp.arange(tile_width, dtype=jnp.int32)
    above_diag = offsets[:, None] < offsets[None, :]
    kept_mask = occupied[:, None, None] & ((row_ids != col_ids)[:, None, None] | above_diag[None])
    squared = jnp.zeros(dissim.shape, jnp.float32)
    for component in range(3):
        spread = row_points[:, component, :, None] - col_points[:, component, None, :]
        squared = squared + spread * spread
    distance = jnp.sqrt(jnp.maximum(squared, distance_floor))
    ratios = jnp.where(kept_mask, dissim / distance, jnp.float32(0.0))
    misfit = jnp.where(kept_mask, (dissim - distance) ** 2, jnp.float32(0.0))
    stress = jnp.sum(misfit)
    row_total = jnp.sum(ratios, axis=2)
    col_total = jnp.sum(ratios, axis=1)
    row_terms = row_points * row_total[:, None, :] - jnp.einsum(
        "sij,scj->sci", ratios, col_points, precision=lax.Precision.HIGHEST
    )
    col_terms = col_points * col_total[:, None, :] - jnp.einsum(
        "sij,sci->scj", ratios, row_points, precision=lax.Precision.HIGHEST
    )
    block_count = coords_all.shape[0]
    totals = jnp.zeros((block_count, 3, tile_width), jnp.float32)
    totals = totals.at[row_slot].add(row_terms).at[col_slot].add(col_terms)
    return (totals, stress)


def local(dissim, tile_map, owned_blocks, start_coords):
    order_list = whole_of(owned_blocks, (("tiles_0", "tiles_1"), "tiles_2"), 0)
    block_count = order_list.shape[0]
    tile_width = dissim.shape[1]
    scaling = jnp.float32(block_count * tile_width)
    slot_of = (
        jnp.zeros((block_count,), jnp.int32)
        .at[order_list]
        .set(jnp.arange(block_count, dtype=jnp.int32))
    )
    coords_all = whole_of(start_coords, (("tiles_0", "tiles_1"), "tiles_2"), 0)
    stress = jnp.float32(0.0)
    for step in range(ITERS):
        totals, misfit = tile_terms(coords_all, dissim, tile_map, slot_of)
        if step == ITERS - 1:
            stress = over_axes(misfit, TILES_REP)
        coords_all = total_of(totals, (("tiles_0", "tiles_1"), ("tiles_2", "rep"))) / scaling
    owned_count = start_coords.shape[0]
    owned = lax.dynamic_slice_in_dim(
        coords_all, lax.axis_index(TILES) * owned_count, owned_count, 0
    )
    return (owned, stress)


def solution(mesh):
    finer = Mesh(
        mesh.devices.reshape(8, 8, 2, mesh.shape["rep"]), ("tiles_0", "tiles_1", "tiles_2", "rep")
    )
    placed = (P(TILES_REP, None, None), P(TILES_REP, None), P(TILES), P(TILES, None, None))
    return jax.shard_map(
        local, mesh=finer, in_specs=placed, out_specs=(P(TILES, None, None), P()), check_vma=False
    )
```

profile of v0, /device:TPU:8, one launch (start us, length us, event | category | flops | bytes accessed | tf_op | source)
XLA Modules:
  0.0 301.4 jit_solution(640555771799460790)
XLA Ops:
  1.4 0.6 broadcast_in_dim.27
  2.1 16.6 %all-to-all-start = ((s32[64,1,1]{2,1,0:T(1,128)}), s32[64,1,1]{2,1,0:T(1,128)S(1)}, u32[]{:S(2)}, u32[]{:S(2)}) async-start(s32[64,1,1]{2,1,0:T(1,128)} %broadcast_in_dim.27), calls=%async_computation | async-start | bytes 65536 | tf_op jit(solution)/shard_map/all_to_all | solution.py:19
  18.6 0.8 maximum_bitcast_fusion
  19.4 0.8 compare_bitcast_fusion.1
  20.2 0.7 copy.116
  20.9 8.8 %all-to-all-done = s32[64,1,1]{2,1,0:T(1,128)S(1)} async-done(((s32[64,1,1]{2,1,0:T(1,128)}), s32[64,1,1]{2,1,0:T(1,128)S(1)}, u32[]{:S(2)}, u32[]{:S(2)}) %all-to-all-start) | async-done | bytes 288 | tf_op jit(solution)/shard_map/all_to_all | solution.py:19
  29.7 1.2 reduce.3
  30.9 3.7 %all_to_all.111 = s32[2,64,1]{1,2,0:T(1,128)S(1)} all-to-all(s32[2,64,1]{1,2,0:T(1,128)S(1)} %broadcast_in_dim.28), channel_id=1, replica_groups=mesh['tiles_0'=8,'tiles_1'=8,'tiles_2'=2,'rep'=4] {'tiles_2'}, dimensions={0} | all-to-all | bytes 1024 | tf_op jit(solution)/shard_map/all_to_all | solution.py:19
  34.6 0.7 broadcast_in_dim.29
  35.3 5.5 %all-to-all-start.2 = ((f32[64,1,3,128]{3,1,2,0:T(1,128)}), f32[64,1,3,128]{3,1,2,0:T(1,128)S(1)}, u32[]{:S(2)}, u32[]{:S(2)}) async-start(f32[64,1,3,128]{3,1,2,0:T(1,128)} %broadcast_in_dim.29), calls=%async_computation.2 | async-start | bytes 196608 | tf_op jit(solution)/shard_map/all_to_all | solution.py:19
  41.1 1.0 scatter_custom_fusion
  42.0 0.8 gather_fusion.2
  42.8 0.8 gather_fusion
  43.6 9.1 %all-to-all-done.2 = f32[64,1,3,128]{3,1,2,0:T(1,128)S(1)} async-done(((f32[64,1,3,128]{3,1,2,0:T(1,128)}), f32[64,1,3,128]{3,1,2,0:T(1,128)S(1)}, u32[]{:S(2)}, u32[]{:S(2)}) %all-to-all-start.2) | async-done | bytes 98336 | tf_op jit(solution)/shard_map/all_to_all | solution.py:19
  52.8 4.0 %all_to_all.112 = f32[2,64,1,3,128]{4,1,3,2,0:T(8,128)S(1)} all-to-all(f32[2,64,1,3,128]{4,1,3,2,0:T(8,128)S(1)} %broadcast_in_dim.30), channel_id=1, replica_groups=mesh['tiles_0'=8,'tiles_1'=8,'tiles_2'=2,'rep'=4] {'tiles_2'}, dimensions={0} | all-to-all | bytes 393216 | tf_op jit(solution)/shard_map/all_to_all | solution.py:19
  56.8 0.2 copy.48
  57.1 0.6 gather_fusion.3
  57.8 0.6 gather_fusion.1
  58.5 3.3 %fusion.7 = (f32[34,128]{1,0:T(8,128)S(1)}, f32[34,128]{1,0:T(8,128)S(1)}, f32[34,128,128]{2,1,0:T(8,128)S(1)}) fusion(f32[34,128,128]{2,1,0:T(8,128)S(1)} %copy-done, f32[34,128]{1,0:T(8,128)S(1)} %bitcast.124, f32[34,128]{1,0:T(8,128)S(1)} %bitcast.128, f32[34,128]{1,0:T(8,128)S(1)} %bitcast.129, f32[34,128]{1,0:T(8,128)S(1)} %bitcast.130, ...), kind=kLoop, calls=%fused_computation.70 | loop fusion | flops 8347136 | bytes 4612164 | tf_op jit(solution)/shard_map/reduce_sum | solution.py:91
  61.8 3.6 %convolution_subtract_fusion.5 = f32[34,3,128]{2,1,0:T(4,128)S(1)} fusion(f32[34,3,128]{2,1,0:T(4,128)S(1)} %gather_fusion.3, f32[34,128,128]{2,1,0:T(8,128)S(1)} %get-tuple-element.22, f32[34,3,128]{2,1,0:T(4,128)S(1)} %gather_fusion.1, f32[34,128]{1,0:T(8,128)S(1)} %get-tuple-element.19), kind=kOutput, calls=%fused_computation.26 | convolution fusion | flops 20080128 | bytes 2402304 | tf_op jit(solution)/shard_map/sij,scj->sci/dot_general | solution.py:92
  65.4 2.0 convolution_subtract_fusion.4
  67.4 2.3 scatter_fusion
  69.7 2.3 scatter_fusion.1
  72.0 0.2 reshape_reshape_reshape.12
  72.2 11.0 %all_to_all.118 = f32[8,64,96]{2,1,0:T(8,128)S(1)} all-to-all(f32[8,64,96]{2,1,0:T(8,128)S(1)} %copy.51), channel_id=1, replica_groups=mesh['tiles_0'=8,'tiles_1'=8,'tiles_2'=2,'rep'=4] {'tiles_2','rep'}, dimensions={0} | all-to-all | bytes 393216 | tf_op jit(solution)/shard_map/all_to_all | solution.py:46
  83.2 15.6 %all_to_all.119 = f32[64,1,96]{2,1,0:T(1,128)S(1)} all-to-all(f32[64,1,96]{2,1,0:T(1,128)S(1)} %bitcast.118), channel_id=1, replica_groups=mesh['tiles_0'=8,'tiles_1'=8,'tiles_2'=2,'rep'=4] {'tiles_0','tiles_1'}, dimensions={0} | all-to-all | bytes 49152 | tf_op jit(solution)/shard_map/all_to_all | solution.py:53
  99.0 15.8 %all_to_all.113 = f32[64,1,96]{2,1,0:T(1,128)S(1)} all-to-all(f32[64,1,96]{2,1,0:T(1,128)S(1)} %broadcast_in_dim.32), channel_id=1, replica_groups=mesh['tiles_0'=8,'tiles_1'=8,'tiles_2'=2,'rep'=4] {'tiles_0','tiles_1'}, dimensions={0} | all-to-all | bytes 49152 | tf_op jit(solution)/shard_map/all_to_all | solution.py:19
  114.8 10.0 %all_to_all.114 = f32[8,64,96]{2,1,0:T(8,128)S(1)} all-to-all(f32[8,64,96]{2,1,0:T(8,128)S(1)} %broadcast_in_dim.33), channel_id=1, replica_groups=mesh['tiles_0'=8,'tiles_1'=8,'tiles_2'=2,'rep'=4] {'tiles_2','rep'}, dimensions={0} | all-to-all | bytes 393216 | tf_op jit(solution)/shard_map/all_to_all | solution.py:19
  124.8 0.2 copy.52
  125.0 0.2 div.33
  125.1 0.6 gather_fusion.4
  125.7 0.6 gather_fusion.5
  126.5 3.3 %fusion.6 = (f32[34,128]{1,0:T(8,128)S(1)}, f32[34,128]{1,0:T(8,128)S(1)}, f32[34,128,128]{2,1,0:T(8,128)S(1)}) fusion(f32[34,128,128]{2,1,0:T(8,128)S(1)} %copy-done, f32[34,128]{1,0:T(8,128)S(1)} %bitcast.135, f32[34,128]{1,0:T(8,128)S(1)} %bitcast.127, f32[34,128]{1,0:T(8,128)S(1)} %bitcast.132, f32[34,128]{1,0:T(8,128)S(1)} %bitcast.125, ...), kind=kLoop, calls=%fused_computation.69 | loop fusion | flops 8347136 | bytes 4612164 | tf_op jit(solution)/shard_map/reduce_sum | solution.py:91
  129.8 2.0 convolution_subtract_fusion.2
  131.8 3.6 %convolution_subtract_fusion.3 = f32[34,3,128]{2,1,0:T(4,128)S(1)} fusion(f32[34,3,128]{2,1,0:T(4,128)S(1)} %gather_fusion.5, f32[34,128,128]{2,1,0:T(8,128)S(1)} %get-tuple-element.21, f32[34,3,128]{2,1,0:T(4,128)S(1)} %gather_fusion.4, f32[34,128]{1,0:T(8,128)S(1)} %get-tuple-element.17), kind=kOutput, calls=%fused_computation.24 | convolution fusion | flops 20080128 | bytes 2402304 | tf_op jit(solution)/shard_map/sij,scj->sci/dot_general | solution.py:92
  135.4 2.3 scatter_fusion.2
  137.7 2.3 scatter_fusion.3
  140.0 0.2 reshape_reshape_reshape.13
  140.2 9.7 %all_to_all.120 = f32[8,64,96]{2,1,0:T(8,128)S(1)} all-to-all(f32[8,64,96]{2,1,0:T(8,128)S(1)} %copy.53), channel_id=1, replica_groups=mesh['tiles_0'=8,'tiles_1'=8,'tiles_2'=2,'rep'=4] {'tiles_2','rep'}, dimensions={0} | all-to-all | bytes 393216 | tf_op jit(solution)/shard_map/all_to_all | solution.py:46
  149.9 15.8 %all_to_all.121 = f32[64,1,96]{2,1,0:T(1,128)S(1)} all-to-all(f32[64,1,96]{2,1,0:T(1,128)S(1)} %bitcast.120), channel_id=1, replica_groups=mesh['tiles_0'=8,'tiles_1'=8,'tiles_2'=2,'rep'=4] {'tiles_0','tiles_1'}, dimensions={0} | all-to-all | bytes 49152 | tf_op jit(solution)/shard_map/all_to_all | solution.py:53
  165.8 15.8 %all_to_all.115 = f32[64,1,96]{2,1,0:T(1,128)S(1)} all-to-all(f32[64,1,96]{2,1,0:T(1,128)S(1)} %broadcast_in_dim.34), channel_id=1, replica_groups=mesh['tiles_0'=8,'tiles_1'=8,'tiles_2'=2,'rep'=4] {'tiles_0','tiles_1'}, dimensions={0} | all-to-all | bytes 49152 | tf_op jit(solution)/shard_map/all_to_all | solution.py:19
  181.7 10.0 %all_to_all.116 = f32[8,64,96]{2,1,0:T(8,128)S(1)} all-to-all(f32[8,64,96]{2,1,0:T(8,128)S(1)} %broadcast_in_dim.35), channel_id=1, replica_groups=mesh['tiles_0'=8,'tiles_1'=8,'tiles_2'=2,'rep'=4] {'tiles_2','rep'}, dimensions={0} | all-to-all | bytes 393216 | tf_op jit(solution)/shard_map/all_to_all | solution.py:19
  191.7 0.2 copy.54
  191.9 0.2 div.37
  192.0 0.6 gather_fusion.6
  192.6 0.6 gather_fusion.7
  193.4 4.5 %fusion.5 = (f32[34,128]{1,0:T(8,128)S(1)}, f32[34,128]{1,0:T(8,128)S(1)}, f32[34,128,128]{2,1,0:T(8,128)S(1)}, f32[]{:T(128)}) fusion(f32[34,128,128]{2,1,0:T(8,128)S(1)} %copy-done, f32[34,128]{1,0:T(8,128)S(1)} %bitcast.139, f32[34,128]{1,0:T(8,128)S(1)} %bitcast.136, f32[34,128]{1,0:T(8,128)S(1)} %bitcast.140, f32[34,128]{1,0:T(8,128)S(1)} %bitcast.137, ...), kind=kLoop, calls=%fused_computation.68 | loop fusion | flops 10575359 | bytes 4612168 | tf_op jit(solution)/shard_map/reduce_sum | solution.py:91
  197.9 2.0 convolution_subtract_fusion
  199.9 3.6 %convolution_subtract_fusion.1 = f32[34,3,128]{2,1,0:T(4,128)S(1)} fusion(f32[34,3,128]{2,1,0:T(4,128)S(1)} %gather_fusion.7, f32[34,128,128]{2,1,0:T(8,128)S(1)} %get-tuple-element.20, f32[34,3,128]{2,1,0:T(4,128)S(1)} %gather_fusion.6, f32[34,128]{1,0:T(8,128)S(1)} %get-tuple-element.15), kind=kOutput, calls=%fused_computation.22 | convolution fusion | flops 20080128 | bytes 2402304 | tf_op jit(solution)/shard_map/sij,scj->sci/dot_general | solution.py:92
  203.5 2.3 scatter_fusion.4
  205.8 2.3 scatter_fusion.5
  208.1 0.2 reshape_reshape_reshape.14
  208.3 9.7 %all_to_all.122 = f32[8,64,96]{2,1,0:T(8,128)S(1)} all-to-all(f32[8,64,96]{2,1,0:T(8,128)S(1)} %copy.55), channel_id=1, replica_groups=mesh['tiles_0'=8,'tiles_1'=8,'tiles_2'=2,'rep'=4] {'tiles_2','rep'}, dimensions={0} | all-to-all | bytes 393216 | tf_op jit(solution)/shard_map/all_to_all | solution.py:46
  218.0 15.8 %all_to_all.123 = f32[64,1,96]{2,1,0:T(1,128)S(1)} all-to-all(f32[64,1,96]{2,1,0:T(1,128)S(1)} %bitcast.122), channel_id=1, replica_groups=mesh['tiles_0'=8,'tiles_1'=8,'tiles_2'=2,'rep'=4] {'tiles_0','tiles_1'}, dimensions={0} | all-to-all | bytes 49152 | tf_op jit(solution)/shard_map/all_to_all | solution.py:53
  233.9 15.8 %all_to_all.117 = f32[64,1,96]{2,1,0:T(1,128)S(1)} all-to-all(f32[64,1,96]{2,1,0:T(1,128)S(1)} %broadcast_in_dim.36), channel_id=1, replica_groups=mesh['tiles_0'=8,'tiles_1'=8,'tiles_2'=2,'rep'=4] {'tiles_0','tiles_1'}, dimensions={0} | all-to-all | bytes 49152 | tf_op jit(solution)/shard_map/all_to_all | solution.py:19
  249.8 0.7 broadcast_in_dim.37
  250.5 3.4 %all-to-all-start.15 = ((f32[8,64,96]{2,1,0:T(8,128)}), f32[8,64,96]{2,1,0:T(8,128)S(1)}, u32[]{:S(2)}, u32[]{:S(2)}) async-start(f32[8,64,96]{2,1,0:T(8,128)} %broadcast_in_dim.37), calls=%async_computation.15 | async-start | bytes 524288 | tf_op jit(solution)/shard_map/all_to_all | solution.py:19
  253.9 16.2 %psum.28 = f32[]{:T(128)} all-reduce(f32[]{:T(128)} %get-tuple-element.23), channel_id=1, replica_groups=mesh['tiles_0'=8,'tiles_1'=8,'tiles_2'=2,'rep'=4] {'tiles_0'}, use_global_device_ids=true, to_apply=%region_20.21 | all-reduce | flops 1 | bytes 8 | tf_op jit(solution)/shard_map/psum | solution.py:36
  270.1 15.4 %psum.29 = f32[]{:T(128)} all-reduce(f32[]{:T(128)} %psum.28), channel_id=1, replica_groups=mesh['tiles_0'=8,'tiles_1'=8,'tiles_2'=2,'rep'=4] {'tiles_1'}, use_global_device_ids=true, to_apply=%region_21.22 | all-reduce | flops 1 | bytes 8 | tf_op jit(solution)/shard_map/psum | solution.py:36
  285.5 3.1 %psum.30 = f32[]{:T(128)} all-reduce(f32[]{:T(128)} %psum.29), channel_id=1, replica_groups=mesh['tiles_0'=8,'tiles_1'=8,'tiles_2'=2,'rep'=4] {'tiles_2'}, use_global_device_ids=true, to_apply=%region_22.23 | all-reduce | flops 1 | bytes 8 | tf_op jit(solution)/shard_map/psum | solution.py:36
  288.5 11.4 %psum.31 = f32[]{:T(128)} all-reduce(f32[]{:T(128)} %psum.30), channel_id=1, replica_groups=mesh['tiles_0'=8,'tiles_1'=8,'tiles_2'=2,'rep'=4] {'rep'}, use_global_device_ids=true, to_apply=%region_23.24 | all-reduce | flops 1 | bytes 8 | tf_op jit(solution)/shard_map/psum | solution.py:36
  300.0 0.2 copy.56
  300.2 0.2 div.41
  300.4 0.6 copy.57
  (62 shorter events, 1.5 us)
Async XLA Ops:
  0.6 57.9 %copy-start = (f32[34,128,128]{2,1,0:T(8,128)S(1)}, f32[34,128,128]{2,1,0:T(8,128)}, u32[]{:S(2)}) copy-start(f32[34,128,128]{2,1,0:T(8,128)} %param.4) | copy-start | bytes 6684676
  2.1 27.6 %all-to-all-start = ((s32[64,1,1]{2,1,0:T(1,128)}), s32[64,1,1]{2,1,0:T(1,128)S(1)}, u32[]{:S(2)}, u32[]{:S(2)}) async-start(s32[64,1,1]{2,1,0:T(1,128)} %broadcast_in_dim.27), calls=%async_computation | async-start | bytes 65536 | tf_op jit(solution)/shard_map/all_to_all | solution.py:19
  35.3 17.5 %all-to-all-start.2 = ((f32[64,1,3,128]{3,1,2,0:T(1,128)}), f32[64,1,3,128]{3,1,2,0:T(1,128)S(1)}, u32[]{:S(2)}, u32[]{:S(2)}) async-start(f32[64,1,3,128]{3,1,2,0:T(1,128)} %broadcast_in_dim.29), calls=%async_computation.2 | async-start | bytes 196608 | tf_op jit(solution)/shard_map/all_to_all | solution.py:19
  250.5 49.5 %all-to-all-start.15 = ((f32[8,64,96]{2,1,0:T(8,128)}), f32[8,64,96]{2,1,0:T(8,128)S(1)}, u32[]{:S(2)}, u32[]{:S(2)}) async-start(f32[8,64,96]{2,1,0:T(8,128)} %broadcast_in_dim.37), calls=%async_computation.15 | async-start | bytes 524288 | tf_op jit(solution)/shard_map/all_to_all | solution.py:19
where the time goes:
time: 306 us; the launch traced here: 301 us
  blocking collectives  199 us (65%)
  other arithmetic  27.9 us (9%)
  starting transfers between devices  25.5 us (8%)
  waiting for transfers between devices  18 us (6%)
  matrix products  16.6 us (5%)
  local copies, waits for them, and re-layouts  12.2 us (4%)
    all_to_all x7, blocking collectives, from_everyone(): return lax.all_to_all(copies, axis, split_axis=0, concat_axis=0, tiled=True)  75.2 us
    all_to_all x3, blocking collectives, sum_by_axis(): return jnp.sum(lax.all_to_all(own, far, 0, 0, tiled=True), axis=0)  47.2 us
    psum x4, blocking collectives, over_axes(): return functools.reduce(lax.psum, axes, array)  46.1 us
    all_to_all x3, blocking collectives, summed_on_arrival(): parts = lax.all_to_all(cut_along(array, dim, peers), axis, 0, 0, tiled=True)  30.4 us
    all_to_all x3, starting transfers between devices, from_everyone(): return lax.all_to_all(copies, axis, split_axis=0, concat_axis=0, tiled=True)  25.5 us
    all_to_all x3, waiting for transfers between devices, from_everyone(): return lax.all_to_all(copies, axis, split_axis=0, concat_axis=0, tiled=True)  18 us
    scatter-add x6, other arithmetic, tile_terms(): totals = totals.at[row_slot].add(row_terms).at[col_slot].add(col_terms)  13.6 us
    reduce_sum x3, other arithmetic, tile_terms(): col_total = jnp.sum(ratios, axis=1)  11.1 us
  transfers between devices with their start and end apart: 3, of which 2 were waited for; matrix products, arithmetic and copies ran while one was open for 2% of the time, Pallas kernels for 0%

commit v1 on v0

v1 whole, which is shorter than its diff:
```python
import functools

import jax
import jax.numpy as jnp
from jax import lax
from jax.experimental import pallas as pl
from jax.experimental.pallas import tpu as pltpu
from jax.sharding import PartitionSpec as P

MESH = pl.DeviceIdType.MESH
F32, BF16 = jnp.float32, jnp.bfloat16
ITERS = 3
FLOOR = 0.25
Q = 24


def pieces(v):
    a = v.astype(BF16)
    rest = v - a.astype(F32)
    b = rest.astype(BF16)
    c = (rest - b.astype(F32)).astype(BF16)
    return a, b, c


def ring_order(n):
    return sorted(range(n), key=lambda d: -min(d, n - d))


def dot(a, b, dims=((1,), (0,))):
    return lax.dot_general(a, b, (dims, ((), ())), preferred_element_type=F32)


def kernel(sizes, dissim, map_v, map_s, owned, start, coords_out, stress_out, *scratch):
    nx, ny, nz, slots, wide = sizes
    (tiles, xs, grid, c_in, half, z_in, y_in, x_in, first, side_a, side_b, sum_a, sum_b, full, hot, hot_t,
     s_core, s_z, s_y, s_x, load_sem,
     f_send, f_recv, cs, cr, zs, zr, ys, yr, xsd, xrv, ags, agr, acs, acr,
     scs, scr, szs, szr, sys_, syr, sxs, sxr) = scratch
    pad = side_a.shape[0]
    blk = 128
    count = 2 * nz * ny
    t = lax.axis_index("tiles")
    x = lax.axis_index("rep")
    y = t // (2 * nz)
    z = (t // 2) % nz
    core = t % 2
    mine = core * nz + z

    def at(x_, y_, z_, c_):
        return {"tiles": (y_ * nz + z_) * 2 + c_, "rep": x_}

    partner = at(x, y, z, 1 - core)

    def z_peer(d):
        return at(x, y, (z + d) % nz, core)

    def y_peer(d):
        return at(x, (y + d) % ny, z, core)

    def x_peer(d):
        return at((x + d) % nx, y, z, core)

    def send(src, dst, send_sem, recv_sem, peer):
        copy = pltpu.make_async_remote_copy(
            src_ref=src, dst_ref=dst, send_sem=send_sem, recv_sem=recv_sem, device_id=peer, device_id_type=MESH
        )
        copy.start()
        return copy

    z_far, y_far, x_far = ring_order(nz), ring_order(ny), ring_order(nx)

    load = pltpu.make_async_copy(dissim, tiles, load_sem)
    load.start()

    barrier = pltpu.get_barrier_semaphore()
    peers = [partner] + [z_peer(d) for d in range(1, nz)]
    peers += [y_peer(d) for d in range(1, ny)] + [x_peer(d) for d in range(1, nx)]
    for peer in peers:
        pl.semaphore_signal(barrier, inc=1, device_id=peer, device_id_type=MESH)

    first[y, pl.ds(0, 3), :] = start[0]
    first[y, pl.ds(3, 1), :] = jnp.full((1, blk), owned[0].astype(F32))
    first[y, pl.ds(4, 4), :] = jnp.zeros((4, blk), F32)
    pl.semaphore_wait(barrier, len(peers))

    sends = [send(first.at[y], first.at[y], f_send.at[d], f_recv.at[d], y_peer(d)) for d in y_far if d]

    ones = jnp.ones((pad, blk), F32)
    for q in range(18, 21):
        side_b[:, q, :] = ones
        side_a[:, q + 3, :] = ones
    for s in range(slots, pad):
        sum_a[s] = jnp.zeros((Q, blk), F32)
        sum_b[s] = jnp.zeros((Q, blk), F32)
    hot[...] = jnp.zeros((2 * pad, count), F32)

    load.wait()
    above = lax.broadcasted_iota(jnp.int32, (blk, blk), 0) < lax.broadcasted_iota(jnp.int32, (blk, blk), 1)

    def drop(s, carry):
        row, col = map_s[s, 0], map_s[s, 1]
        occupied = row >= 0
        upper = jnp.where(occupied, F32(1), F32(0))
        lower = jnp.where(occupied & (row != col), F32(1), F32(0))
        tiles[s] = tiles[s] * jnp.where(above, upper, lower)
        return carry

    lax.fori_loop(0, slots, drop, 0)

    for copy in sends:
        copy.wait_recv()
    for c in range(4):
        xs[mine, c] = first[:, c, :]
    for copy in sends:
        copy.wait_send()

    def gather_all(planes):
        own = xs.at[mine, pl.ds(0, planes)]
        out = [send(own, own, ags.at[d], agr.at[d], z_peer(d)) for d in z_far if d]
        across = {0: send(own, own, acs.at[0], acr.at[0], partner)}
        for copy, d in reversed(list(zip(out, [d for d in z_far if d]))):
            copy.wait_recv()
            came = xs.at[core * nz + (z - d + nz) % nz, pl.ds(0, planes)]
            across[d] = send(came, came, acs.at[d], acr.at[d], partner)
        for copy in across.values():
            copy.wait_recv()
        for copy in out + list(across.values()):
            copy.wait_send()

    gather_all(4)

    order = xs[:, 3].reshape(count, blk)
    order_row = jnp.transpose(order)
    ids = map_v[...].astype(F32)
    hot[pl.ds(0, slots), :] = jnp.where(ids[:, 0:1] == order_row[0:1], F32(1), F32(0))
    hot[pl.ds(pad, slots), :] = jnp.where(ids[:, 1:2] == order_row[0:1], F32(1), F32(0))
    hot_t[...] = jnp.transpose(hot[...])

    for step in range(ITERS):
        last = step == ITERS - 1

        pick = hot[...].astype(BF16)
        norm = jnp.zeros((2 * pad, blk), F32)
        for c in range(3):
            parts = [dot(pick, v) for v in pieces(xs[:, c].reshape(count, blk))]
            value = parts[0] + parts[1] + parts[2]
            full[c] = value
            norm = norm + value * value
            for q, (a, b) in enumerate(((0, 0), (0, 1), (1, 0), (1, 1), (0, 2), (2, 0))):
                side_a[:, 6 * c + q, :] = parts[a][:pad]
                side_b[:, 6 * c + q, :] = -2.0 * parts[b][pad:]
        for q, v in enumerate(pieces(norm)):
            side_a[:, 18 + q, :] = v.astype(F32)[:pad]
            side_b[:, 21 + q, :] = v.astype(F32)[pad:]

        def tile(s, stress):
            a = side_a[s].astype(BF16)
            b = side_b[s].astype(BF16)
            squared = jnp.maximum(dot(a, b, ((0,), (0,))), FLOOR)
            inverse = lax.rsqrt(squared)
            delta = tiles[s]
            ratio = delta * inverse
            high = ratio.astype(BF16)
            low = (ratio - high.astype(F32)).astype(BF16)
            sum_a[s] = dot(a, high) + dot(a, low)
            sum_b[s] = dot(b, high, ((1,), (1,))) + dot(b, low, ((1,), (1,)))
            if last:
                misfit = jnp.where(delta > 0.0, delta - squared * inverse, F32(0))
                stress = stress + jnp.sum((misfit * misfit).reshape(blk // 8, 8, blk), axis=0)
            return stress

        stress = lax.fori_loop(0, slots, tile, jnp.zeros((8, blk), F32))

        drop_t = hot_t[...].astype(BF16)
        row_total, col_total = sum_b[:, 18, :], sum_a[:, 21, :]
        for c in range(3):
            row_sum = -0.5 * (sum_b[:, 6 * c, :] + sum_b[:, 6 * c + 1, :] + sum_b[:, 6 * c + 4, :])
            col_sum = sum_a[:, 6 * c, :] + sum_a[:, 6 * c + 2, :] + sum_a[:, 6 * c + 5, :]
            points = full[c]
            terms = jnp.concatenate([points[:pad] * row_total - row_sum, points[pad:] * col_total - col_sum], axis=0)
            total = functools.reduce(jnp.add, [dot(drop_t, v) for v in pieces(terms)])
            grid[:, c] = total.reshape(2 * nz, ny, blk)

        crossing = {}
        for d in z_far:
            to = (z + d) % nz
            crossing[d] = send(grid.at[(1 - core) * nz + to], c_in.at[to], cs.at[d], cr.at[d], partner)
        waits = list(crossing.values())
        if last:
            s_core[core] = jnp.sum(stress, axis=0, keepdims=True)
            small = send(s_core.at[core], s_core.at[core], scs, scr, partner)
            waits.append(small)
        along = []
        for d in z_far:
            to = (z + d) % nz
            crossing[d].wait_recv()
            if d:
                half[to] = grid[core * nz + to] + c_in[to]
                along.append(send(half.at[to], z_in.at[z], zs.at[d], zr.at[d], z_peer(d)))
            else:
                z_in[z] = grid[mine] + c_in[z]
        if last:
            small.wait_recv()
            s_z[z] = s_core[0] + s_core[1]
            along += [send(s_z.at[z], s_z.at[z], szs.at[d], szr.at[d], z_peer(d)) for d in z_far if d]
        for copy in along:
            copy.wait_recv()
        waits += along

        y_in[step, y] = functools.reduce(jnp.add, [z_in[k] for k in range(nz)])
        own = y_in.at[step, y]
        along = [send(own, own, ys.at[step, d], yr.at[step, d], y_peer(d)) for d in y_far if d]
        if last:
            s_y[y] = functools.reduce(jnp.add, [s_z[k] for k in range(nz)])
            along += [send(s_y.at[y], s_y.at[y], sys_.at[d], syr.at[d], y_peer(d)) for d in y_far if d]
        for copy in along:
            copy.wait_recv()
        waits += along

        x_in[step, x] = functools.reduce(jnp.add, [y_in[step, k] for k in range(ny)])
        own = x_in.at[step, x]
        along = [send(own, own, xsd.at[step, d], xrv.at[step, d], x_peer(d)) for d in x_far if d]
        if last:
            s_x[x] = functools.reduce(jnp.add, [s_y[k] for k in range(ny)])
            along += [send(s_x.at[x], s_x.at[x], sxs.at[d], sxr.at[d], x_peer(d)) for d in x_far if d]
        for copy in along:
            copy.wait_recv()
        waits += along

        if last:
            for c in range(3):
                rows = functools.reduce(jnp.add, [x_in[step, k, c, pl.ds(y, 1), :] for k in range(nx)])
                coords_out[0, pl.ds(c, 1), :] = rows * F32(1.0 / (count * blk))
            stress_out[0, 0] = jnp.sum(functools.reduce(jnp.add, [s_x[k] for k in range(nx)]))
        else:
            piece = functools.reduce(jnp.add, [x_in[step, k] for k in range(nx)])
            xs[mine, pl.ds(0, 3)] = piece * F32(1.0 / (count * blk))
            gather_all(3)
        for copy in waits:
            copy.wait_send()


def local(sizes, dissim, tile_map, owned_blocks, start_coords):
    nx, ny, nz, slots, wide = sizes
    blk = dissim.shape[1]
    pad = -(-slots // 8) * 8
    count = 2 * nz * ny
    dma = pltpu.SemaphoreType.DMA
    vmem = lambda *shape: pltpu.VMEM(shape, F32)
    coords, stress = pl.pallas_call(
        functools.partial(kernel, sizes),
        out_shape=(
            jax.ShapeDtypeStruct((1, 3, blk), F32),
            jax.ShapeDtypeStruct((1, 1), F32),
        ),
        in_specs=[
            pl.BlockSpec(memory_space=pl.ANY),
            pl.BlockSpec(memory_space=pltpu.VMEM),
            pl.BlockSpec(memory_space=pltpu.SMEM),
            pl.BlockSpec(memory_space=pltpu.SMEM),
            pl.BlockSpec(memory_space=pltpu.VMEM),
        ],
        out_specs=(
            pl.BlockSpec(memory_space=pltpu.VMEM),
            pl.BlockSpec(memory_space=pltpu.SMEM),
        ),
        scratch_shapes=[
            vmem(slots, blk, blk),
            vmem(2 * nz, 4, ny, blk),
            vmem(2 * nz, 3, ny, blk),
            vmem(nz, 3, ny, blk),
            vmem(nz, 3, ny, blk),
            vmem(nz, 3, ny, blk),
            vmem(ITERS, ny, 3, ny, blk),
            vmem(ITERS, nx, 3, ny, blk),
            vmem(ny, 8, blk),
            vmem(pad, Q, blk),
            vmem(pad, Q, blk),
            vmem(pad, Q, blk),
            vmem(pad, Q, blk),
            vmem(3, 2 * pad, blk),
            vmem(2 * pad, count),
            vmem(count, 2 * pad),
            vmem(2, 1, blk),
            vmem(nz, 1, blk),
            vmem(ny, 1, blk),
            vmem(nx, 1, blk),
            dma,
            dma((ny,)), dma((ny,)),
            dma((nz,)), dma((nz,)),
            dma((nz,)), dma((nz,)),
            dma((ITERS, ny)), dma((ITERS, ny)),
            dma((ITERS, nx)), dma((ITERS, nx)),
            dma((nz,)), dma((nz,)),
            dma((nz,)), dma((nz,)),
            dma, dma,
            dma((nz,)), dma((nz,)),
            dma((ny,)), dma((ny,)),
            dma((nx,)), dma((nx,)),
        ],
        compiler_params=pltpu.CompilerParams(
            collective_id=0, has_side_effects=True, vmem_limit_bytes=32 * 2**20
        ),
        name="guttman",
    )(dissim, tile_map, tile_map, owned_blocks, start_coords)
    return coords, stress.reshape(())


def build(mesh, ny, nz, slots):
    nx = mesh.shape["rep"]
    sizes = (nx, ny, nz, slots, 0)
    both = ("tiles", "rep")
    return jax.shard_map(
        functools.partial(local, sizes),
        mesh=mesh,
        in_specs=(P(both, None, None), P(both, None), P("tiles"), P("tiles", None, None)),
        out_specs=(P("tiles", None, None), P()),
        check_vma=False,
    )


def solution(mesh):
    return build(mesh, 8, 8, 34)
```

time: 306 us -> 132 us (0.43); the launches traced: 301 us -> 132 us
  blocking collectives: 199 us -> 0 us
  Pallas kernels: 0 us -> 125 us
  other arithmetic: 27.9 us -> 0 us
  starting transfers between devices: 25.5 us -> 0 us
  waiting for transfers between devices: 18 us -> 0 us
  matrix products: 16.6 us -> 0 us
  local copies, waits for them, and re-layouts: 12.2 us -> 3.65 us
    all_to_all x13 -> x0, blocking collectives: 153 us -> none  [the longest x7 75.2 us: from_everyone(): return lax.all_to_all(copies, axis, split_axis=0, concat_axis=0, tiled=True)]
    pallas_call x0 -> x1, Pallas kernels: none -> 125 us  [local(): pl.pallas_call(functools.partial(kernel, sizes), out_shape=(jax.ShapeDtyp...]
    psum x4 -> x0, blocking collectives: 46.1 us -> none  [over_axes(): return functools.reduce(lax.psum, axes, array)]
    all_to_all x3 -> x0, starting transfers between devices: 25.5 us -> none  [from_everyone(): return lax.all_to_all(copies, axis, split_axis=0, concat_axis=0, tiled=True)]
    all_to_all x3 -> x0, waiting for transfers between devices: 18 us -> none  [from_everyone(): return lax.all_to_all(copies, axis, split_axis=0, concat_axis=0, tiled=True)]
    dot_general x6 -> x0, matrix products: 16.6 us -> none  [the longest x3 10.7 us: tile_terms(): jnp.einsum('sij,scj->sci', ratios, col_points, precision=lax.Precision.HI...]
    scatter-add x6 -> x0, other arithmetic: 13.6 us -> none  [tile_terms(): totals = totals.at[row_slot].add(row_terms).at[col_slot].add(col_terms)]
    reduce_sum x9 -> x0, other arithmetic: 11.4 us -> none  [the longest x3 11.1 us: tile_terms(): col_total = jnp.sum(ratios, axis=1)]
  transfers between devices with their start and end apart: 3 -> 0, of which waited for: 2 -> 0; matrix products, arithmetic and copies ran while one was open for 2% -> 0% of each run, Pallas kernels for 0% -> 0%
where the time goes in v1:
time: 132 us
  Pallas kernels  125 us (95%)
  local copies, waits for them, and re-layouts  3.65 us (3%)
  between operations  3.05 us (2%)
    pallas_call x1, Pallas kernels, local(): pl.pallas_call(functools.partial(kernel, sizes), out_shape=(jax.ShapeDtyp...  125 us
    unnamed x5, local copies, waits for them, and re-layouts  3.65 us

profile of v1, /device:TPU:8, one launch (start us, length us, event | category | flops | bytes accessed | tf_op | source)
XLA Modules:
  0.0 131.7 jit_solution(3460421053641981950)
XLA Ops:
  1.3 0.7 copy.8.start
  2.0 0.8 copy.6.map_v.map_s
  2.7 0.0 copy-start
  2.7 1.6 %copy-done = f32[34,128,128]{2,1,0:T(8,128)S(1)} copy-done((f32[34,128,128]{2,1,0:T(8,128)S(1)}, f32[34,128,128]{2,1,0:T(8,128)}, u32[]{:S(2)}) %copy-start) | copy-done | bytes 2228248
  4.4 125.0 %guttman.1 = (f32[1,3,128]{2,1,0:T(4,128)S(1)}, f32[1,1]{1,0:T(1,128)}) custom-call(f32[34,128,128]{2,1,0:T(8,128)S(1)} %copy-done, s32[34,2]{1,0:T(8,128)S(1)} %copy.6.map_v.map_s, s32[34,2]{1,0:T(8,128)S(1)} %copy.6.map_v.map_s, s32[1]{0:T(128)S(6)} %copy.11.owned, f32[1,3,128]{2,1,0:T(4,128)S(1)} %copy.8.start), custom_call_target="tpu_custom_call" | custom-call | tf_op jit(solution)/shard_map/guttman/pallas_call | solution.py:250
  129.3 0.6 copy.9
Async XLA Ops:
  2.7 1.6 %copy-start = (f32[34,128,128]{2,1,0:T(8,128)S(1)}, f32[34,128,128]{2,1,0:T(8,128)}, u32[]{:S(2)}) copy-start(f32[34,128,128]{2,1,0:T(8,128)} %dissim.1) | copy-start | bytes 6684676

commit v2 on v1

--- a/solution.py
+++ b/solution.py
@@ -31,8 +31,8 @@
 
 
 def kernel(sizes, dissim, map_v, map_s, owned, start, coords_out, stress_out, *scratch):
-    nx, ny, nz, slots, wide = sizes
-    (tiles, xs, grid, c_in, half, z_in, y_in, x_in, first, side_a, side_b, sum_a, sum_b, full, hot, hot_t,
+    nx, ny, nz, slots, unroll = sizes
+    (tiles, tiles_t, xs, grid, c_in, half, z_in, y_in, x_in, first, side_a, side_b, sum_a, sum_b, full, hot_r, hot_c,
      s_core, s_z, s_y, s_x, load_sem,
      f_send, f_recv, cs, cr, zs, zr, ys, yr, xsd, xrv, ags, agr, acs, acr,
      scs, scr, szs, szr, sys_, syr, sxs, sxr) = scratch
@@ -78,7 +78,8 @@
     for peer in peers:
         pl.semaphore_signal(barrier, inc=1, device_id=peer, device_id_type=MESH)
 
-    first[y, pl.ds(0, 3), :] = start[0]
+    for c in range(3):
+        first[y, pl.ds(c, 1), :] = start[c]
     first[y, pl.ds(3, 1), :] = jnp.full((1, blk), owned[0].astype(F32))
     first[y, pl.ds(4, 4), :] = jnp.zeros((4, blk), F32)
     pl.semaphore_wait(barrier, len(peers))
@@ -92,20 +93,23 @@
     for s in range(slots, pad):
         sum_a[s] = jnp.zeros((Q, blk), F32)
         sum_b[s] = jnp.zeros((Q, blk), F32)
-    hot[...] = jnp.zeros((2 * pad, count), F32)
+    hot_r[...] = jnp.zeros((count, blk), F32)
+    hot_c[...] = jnp.zeros((count, blk), F32)
 
     load.wait()
     above = lax.broadcasted_iota(jnp.int32, (blk, blk), 0) < lax.broadcasted_iota(jnp.int32, (blk, blk), 1)
 
     def drop(s, carry):
-        row, col = map_s[s, 0], map_s[s, 1]
+        row, col = map_s[0, s], map_s[1, s]
         occupied = row >= 0
         upper = jnp.where(occupied, F32(1), F32(0))
         lower = jnp.where(occupied & (row != col), F32(1), F32(0))
-        tiles[s] = tiles[s] * jnp.where(above, upper, lower)
+        kept = tiles[s] * jnp.where(above, upper, lower)
+        tiles[s] = kept
+        tiles_t[s] = jnp.transpose(kept)
         return carry
 
-    lax.fori_loop(0, slots, drop, 0)
+    lax.fori_loop(0, slots, drop, 0, unroll=2)
 
     for copy in sends:
         copy.wait_recv()
@@ -129,17 +133,16 @@
 
     gather_all(4)
 
-    order = xs[:, 3].reshape(count, blk)
-    order_row = jnp.transpose(order)
+    order = xs[:, 3].reshape(count, blk)[:, :slots]
     ids = map_v[...].astype(F32)
-    hot[pl.ds(0, slots), :] = jnp.where(ids[:, 0:1] == order_row[0:1], F32(1), F32(0))
-    hot[pl.ds(pad, slots), :] = jnp.where(ids[:, 1:2] == order_row[0:1], F32(1), F32(0))
-    hot_t[...] = jnp.transpose(hot[...])
+    hot_r[:, pl.ds(0, slots)] = jnp.where(order == ids[0:1], F32(1), F32(0))
+    hot_c[:, pl.ds(0, slots)] = jnp.where(order == ids[1:2], F32(1), F32(0))
+    pick = jnp.concatenate([jnp.transpose(hot_r[...])[:pad], jnp.transpose(hot_c[...])[:pad]], axis=0).astype(BF16)
+    put = jnp.concatenate([hot_r[...], hot_c[...]], axis=1).astype(BF16)
 
     for step in range(ITERS):
         last = step == ITERS - 1
 
-        pick = hot[...].astype(BF16)
         norm = jnp.zeros((2 * pad, blk), F32)
         for c in range(3):
             parts = [dot(pick, v) for v in pieces(xs[:, c].reshape(count, blk))]
@@ -156,29 +159,31 @@
         def tile(s, stress):
             a = side_a[s].astype(BF16)
             b = side_b[s].astype(BF16)
-            squared = jnp.maximum(dot(a, b, ((0,), (0,))), FLOOR)
-            inverse = lax.rsqrt(squared)
-            delta = tiles[s]
-            ratio = delta * inverse
-            high = ratio.astype(BF16)
-            low = (ratio - high.astype(F32)).astype(BF16)
-            sum_a[s] = dot(a, high) + dot(a, low)
-            sum_b[s] = dot(b, high, ((1,), (1,))) + dot(b, low, ((1,), (1,)))
-            if last:
-                misfit = jnp.where(delta > 0.0, delta - squared * inverse, F32(0))
-                stress = stress + jnp.sum((misfit * misfit).reshape(blk // 8, 8, blk), axis=0)
+            for near, far, deltas, sums in ((a, b, tiles, sum_a), (b, a, tiles_t, sum_b)):
+                squared = jnp.maximum(dot(near, far, ((0,), (0,))), FLOOR)
+                inverse = lax.rsqrt(squared)
+                delta = deltas[s]
+                ratio = delta * inverse
+                high = ratio.astype(BF16)
+                low = (ratio - high.astype(F32)).astype(BF16)
+                sums[s] = dot(jnp.concatenate([near, near], axis=1), jnp.concatenate([high, low], axis=0))
+                if last and deltas is tiles:
+                    misfit = jnp.where(delta > 0.0, delta - squared * inverse, F32(0))
+                    stress = stress + jnp.sum((misfit * misfit).reshape(blk // 8, 8, blk), axis=0)
             return stress
 
-        stress = lax.fori_loop(0, slots, tile, jnp.zeros((8, blk), F32))
-
-        drop_t = hot_t[...].astype(BF16)
+        stress = lax.fori_loop(0, slots, tile, jnp.zeros((8, blk), F32), unroll=unroll)
+
         row_total, col_total = sum_b[:, 18, :], sum_a[:, 21, :]
         for c in range(3):
             row_sum = -0.5 * (sum_b[:, 6 * c, :] + sum_b[:, 6 * c + 1, :] + sum_b[:, 6 * c + 4, :])
             col_sum = sum_a[:, 6 * c, :] + sum_a[:, 6 * c + 2, :] + sum_a[:, 6 * c + 5, :]
             points = full[c]
-            terms = jnp.concatenate([points[:pad] * row_total - row_sum, points[pad:] * col_total - col_sum], axis=0)
-            total = functools.reduce(jnp.add, [dot(drop_t, v) for v in pieces(terms)])
+            spare = jnp.zeros((blk - pad, blk), F32)
+            row_terms = jnp.concatenate([points[:pad] * row_total - row_sum, spare], axis=0)
+            col_terms = jnp.concatenate([points[pad:] * col_total - col_sum, spare], axis=0)
+            terms = jnp.concatenate([row_terms, col_terms], axis=0)
+            total = functools.reduce(jnp.add, [dot(put, v) for v in pieces(terms)])
             grid[:, c] = total.reshape(2 * nz, ny, blk)
 
         crossing = {}
@@ -230,7 +235,7 @@
         if last:
             for c in range(3):
                 rows = functools.reduce(jnp.add, [x_in[step, k, c, pl.ds(y, 1), :] for k in range(nx)])
-                coords_out[0, pl.ds(c, 1), :] = rows * F32(1.0 / (count * blk))
+                coords_out[c] = rows * F32(1.0 / (count * blk))
             stress_out[0, 0] = jnp.sum(functools.reduce(jnp.add, [s_x[k] for k in range(nx)]))
         else:
             piece = functools.reduce(jnp.add, [x_in[step, k] for k in range(nx)])
@@ -241,7 +246,7 @@
 
 
 def local(sizes, dissim, tile_map, owned_blocks, start_coords):
-    nx, ny, nz, slots, wide = sizes
+    nx, ny, nz, slots, unroll = sizes
     blk = dissim.shape[1]
     pad = -(-slots // 8) * 8
     count = 2 * nz * ny
@@ -250,11 +255,11 @@
     coords, stress = pl.pallas_call(
         functools.partial(kernel, sizes),
         out_shape=(
-            jax.ShapeDtypeStruct((1, 3, blk), F32),
+            jax.ShapeDtypeStruct((3, 1, blk), F32),
             jax.ShapeDtypeStruct((1, 1), F32),
         ),
         in_specs=[
-            pl.BlockSpec(memory_space=pl.ANY),
+            pl.BlockSpec(memory_space=pltpu.HBM),
             pl.BlockSpec(memory_space=pltpu.VMEM),
             pl.BlockSpec(memory_space=pltpu.SMEM),
             pl.BlockSpec(memory_space=pltpu.SMEM),
@@ -265,6 +270,7 @@
             pl.BlockSpec(memory_space=pltpu.SMEM),
         ),
         scratch_shapes=[
+            vmem(slots, blk, blk),
             vmem(slots, blk, blk),
             vmem(2 * nz, 4, ny, blk),
             vmem(2 * nz, 3, ny, blk),
@@ -279,8 +285,8 @@
             vmem(pad, Q, blk),
             vmem(pad, Q, blk),
             vmem(3, 2 * pad, blk),
-            vmem(2 * pad, count),
-            vmem(count, 2 * pad),
+            vmem(count, blk),
+            vmem(count, blk),
             vmem(2, 1, blk),
             vmem(nz, 1, blk),
             vmem(ny, 1, blk),
@@ -299,16 +305,16 @@
             dma((nx,)), dma((nx,)),
         ],
         compiler_params=pltpu.CompilerParams(
-            collective_id=0, has_side_effects=True, vmem_limit_bytes=32 * 2**20
+            collective_id=0, has_side_effects=True, vmem_limit_bytes=63 * 2**20
         ),
         name="guttman",
-    )(dissim, tile_map, tile_map, owned_blocks, start_coords)
-    return coords, stress.reshape(())
+    )(dissim, tile_map.T, tile_map.T, owned_blocks, jnp.swapaxes(start_coords, 0, 1))
+    return jnp.swapaxes(coords, 0, 1), stress.reshape(())
 
 
 def build(mesh, ny, nz, slots):
     nx = mesh.shape["rep"]
-    sizes = (nx, ny, nz, slots, 0)
+    sizes = (nx, ny, nz, slots, next(u for u in (17, 7, 5, 3, 2, 1) if slots % u == 0))
     both = ("tiles", "rep")
     return jax.shard_map(
         functools.partial(local, sizes),

time: 132 us -> 97.3 us (0.74)
  Pallas kernels: 125 us -> 92.8 us
  local copies, waits for them, and re-layouts: 3.65 us -> 1.23 us
    pallas_call x1, Pallas kernels: 125 us -> 92.8 us  [local(): pl.pallas_call(functools.partial(kernel, sizes), out_shape=(jax.ShapeDtyp...]
    unnamed x5 -> x1, local copies, waits for them, and re-layouts: 3.65 us -> 1.23 us
where the time goes in v2:
time: 97.3 us; the launch traced here: 97.1 us
  Pallas kernels  92.8 us (95%)
  between operations  3.05 us (3%)
  local copies, waits for them, and re-layouts  1.23 us (1%)
    pallas_call x1, Pallas kernels, local(): pl.pallas_call(functools.partial(kernel, sizes), out_shape=(jax.ShapeDtyp...  92.8 us

profile of v2, /device:TPU:8, one launch (start us, length us, event | category | flops | bytes accessed | tf_op | source)
XLA Modules:
  0.0 97.1 jit_solution(12601808531036434377)
XLA Ops:
  1.3 92.8 %guttman.1 = (f32[3,1,128]{2,1,0:T(1,128)}, f32[1,1]{1,0:T(1,128)}) custom-call(f32[34,128,128]{2,1,0:T(8,128)} %dissim.1, s32[2,34]{1,0:T(2,128)} %bitcast.4, s32[2,34]{1,0:T(2,128)} %bitcast.5, s32[1]{0:T(128)S(6)} %copy.8.owned, f32[3,1,128]{2,1,0:T(1,128)} %bitcast.6), custom_call_target="tpu_custom_call" | custom-call | tf_op jit(solution)/shard_map/guttman/pallas_call | solution.py:255
  94.1 1.2 %copy.9 = f32[1,3,128]{2,0,1:T(1,128)} copy(f32[1,3,128]{2,0,1:T(1,128)} %bitcast.7) | data formatting | bytes 3072
